TPU v7x, 512 devices: a whole 4x8x8 slice. The times are simulated.
512 devices in a mesh: comp: 2 (over z_lo), lat: 16 (over y, core), lon: 16 (over x, z_hi).
Axes of the slice: x: 4, y: 8, z: 8 (z_hi: 4, z_lo: 2; z = z_hi * 2 + z_lo), core: 2. Of those that a mesh axis runs over, the one named last changes fastest.
Arguments:
- state: float32 [2, 12, 256, 2048], P('comp', None, 'lat', 'lon'), may hold values from -6 to 6
- prev_surface: float32 [2, 256, 2048], P(None, 'lat', 'lon'), may hold values from -6 to 6
- mixing: float32 [2, 11, 256, 2048], P('comp', None, 'lat', 'lon'), may hold values from 0.1 to 3
- velocity: float32 [2, 2, 256, 2048], P('comp', None, 'lat', 'lon'), may hold values from -0.3 to 0.3
- coupling: float32 [2, 256, 2048], P('comp', 'lat', 'lon'), may hold values from 0.1 to 1
- sea_mask: int32 [2, 256, 2048], P('comp', 'lat', 'lon'), may hold values 0 or 1
- interp_index: int32 [2, 4, 256, 2048], P('comp', None, 'lat', 'lon'), may hold values from 0 to 2047
- interp_weight: float32 [2, 4, 256, 2048], P('comp', None, 'lat', 'lon'), may hold values from 0.05 to 0.45
Outputs:
- new_state: float32 [2, 12, 256, 2048], P('comp', None, 'lat', 'lon')
- surface_series: float32 [2, 2, 256, 2048], P('comp', None, 'lat', 'lon')
Inputs may be any that keep to these rules, and one draw needn't show every extreme that they name: `interp_index`: A tile index, r * 128 + c, of a cell in the same latitude-longitude tile.
All inputs are finite; a program needn't handle non-finite values. No bound on the sum of `sea_mask` on one device may be relied on, other than what follows from the above.
Results may differ from a plain program's by a relative error of at most 0.0001.
Values sent between devices are 32-bit elements; how exact they have to be, the bound alone decides.
No kernel may reach another device: no remote copies, remote signals or barrier semaphores. Data moves between devices by JAX's collectives and lax.ppermute only.
A program may use at most 64 MiB of HBM per device.

v0:
```python
import jax
import jax.numpy as jnp
from jax import lax
from jax.experimental import pallas as pl
from jax.experimental.pallas import tpu as pltpu
from jax.sharding import PartitionSpec as P


INTERPRET = False
NSTEP = 2
LEV = 12
ROWS = 16
COLS = 128
smoothing = 0.15

AT_MIX = 4 * LEV
AT_VEL = AT_MIX + 2 * (LEV - 1)
AT_RATE = AT_VEL + 4
AT_WEIGHT = 80
AT_INDEX = 88
AT_FLUX = AT_WEIGHT
AT_WEST = 96
AT_EAST = 100
ROW_MESSAGE = 104
COL_MESSAGE = 2 * ROWS


def lanes(rows):
    return lax.broadcasted_iota(jnp.int32, (rows, COLS), 1)


def sublanes():
    return lax.broadcasted_iota(jnp.int32, (8, COLS), 0)


def roll(x, shift, axis):
    shift %= x.shape[axis]
    return pltpu.roll(x, shift, axis) if shift else x


def gather_cells(table, index):
    sources = [jnp.broadcast_to(table[r : r + 1], (8, COLS)) for r in range(ROWS)]
    blocks = []
    for at in range(0, index.shape[0], 8):
        cell = index[at : at + 8]
        column = lax.bitwise_and(cell, COLS - 1)
        picked = [
            jnp.take_along_axis(source, column, axis=1, mode="promise_in_bounds")
            for source in sources
        ]
        bit = COLS
        while len(picked) > 1:
            chosen = lax.bitwise_and(cell, bit) != 0
            picked = [jnp.where(chosen, b, a) for a, b in zip(picked[::2], picked[1::2])]
            bit *= 2
        blocks.append(picked[0])
    return jnp.concatenate(blocks, axis=0)


def regrid_tile(table, index_ref, weight_ref):
    index = index_ref[...].reshape(4 * ROWS, COLS)
    picked = gather_cells(table, index).reshape(4, ROWS, COLS)
    return jnp.sum(picked * weight_ref[...], axis=0)


def pack_columns(last, state, mix, vel, rate, index, weight, flux, msg):
    lane = lanes(ROWS)

    def packed(at_end):
        total = jnp.zeros((ROWS, COLS), jnp.float32)

        def put(total, x, at, width):
            shift = at - (COLS - width) if at_end else at
            return jnp.where((lane >= at) & (lane < at + width), roll(x, shift, 1), total)

        for level in range(LEV):
            total = put(total, state[level], 4 * level, 4)
        for level in range(LEV - 1):
            total = put(total, mix[level], AT_MIX + 2 * level, 2)
        for part in range(2):
            total = put(total, vel[part], AT_VEL + 2 * part, 2)
        total = put(total, rate[...], AT_RATE, 2)
        for j in range(4):
            total = put(total, weight[j], AT_WEIGHT + 2 * j, 2)
            total = put(total, index[j].astype(jnp.float32), AT_INDEX + 2 * j, 2)
        return total

    @pl.when(last)
    def _():
        msg[0:ROWS] = packed(True)

    @pl.when(jnp.logical_not(last))
    def _():
        msg[0:ROWS] = packed(False)

    msg[ROWS:] = flux[...]


def near_early_kernel(*refs):
    @pl.when(starts_early())
    def _():
        pack_columns(lax.rem(lax.axis_index("lon"), 2) == 0, *refs)


def near_late_kernel(*refs):
    @pl.when(jnp.logical_not(starts_early()))
    def _():
        pack_columns(lax.rem(lax.axis_index("lon"), 2) == 0, *refs)


def pack_columns_kernel(
    state_hbm, prev_hbm, mix_hbm, vel_hbm, couple_hbm, mask_hbm, index_hbm, weight_hbm,
    msg, flux_out, rate_out, state, prev, mix, vel, index, weight, couple, mask, arrived,
):
    moves = [
        pltpu.make_async_copy(source, target, arrived.at[k])
        for k, (source, target) in enumerate(
            (
                (index_hbm, index),
                (prev_hbm, prev),
                (weight_hbm, weight),
                (state_hbm, state),
                (mix_hbm, mix),
                (vel_hbm, vel),
                (couple_hbm, couple),
                (mask_hbm, mask),
            )
        )
    ]
    for move in moves:
        move.start()
    is_atmosphere = lax.axis_index("comp") == 0
    odd = lax.rem(lax.axis_index("lon"), 2) == 1
    for move in moves[:3]:
        move.wait()

    @pl.when(is_atmosphere)
    def _():
        flux_out[...] = regrid_tile(prev[0], index, weight)

    for move in moves[3:]:
        move.wait()
    rate = couple[...] * mask[...].astype(jnp.float32)
    rate_out[...] = rate


    @pl.when(is_atmosphere)
    def _():
        flux_out[...] = rate * (flux_out[...] - state[0])

    @pl.when(jnp.logical_not(is_atmosphere))
    def _():
        flux_out[...] = jnp.zeros((ROWS, COLS), jnp.float32)

    pack_columns(odd, state, mix, vel, rate_out, index, weight, flux_out, msg)


def starts_early():
    return lax.rem(lax.axis_index("lon"), 4) < 2


def sides(near, far):
    odd = lax.rem(lax.axis_index("lon"), 2) == 1
    return jnp.where(odd, near, far), jnp.where(odd, far, near)


def column_messages(got):
    early = starts_early()
    near = jnp.where(early, got[0][...], got[1][...])
    return sides(near, jnp.where(early, got[2][...], got[3][...]))


def pack_rows_kernel(
    state, mix, vel, rate_in, index, weight, flux, early, late, to_early, to_late, msg0, msg1
):
    odd = lax.rem(lax.axis_index("lat"), 2) == 1
    west, east = column_messages((early, late, to_early, to_late))
    rate = rate_in[...]

    def put(x, at, width):
        head, tail = x[0:width], x[ROWS - width : ROWS]
        msg0[at : at + width] = jnp.where(odd, head, tail)
        msg1[at : at + width] = jnp.where(odd, tail, head)

    for level in range(LEV):
        put(state[level], 4 * level, 4)
    for level in range(LEV - 1):
        put(mix[level], AT_MIX + 2 * level, 2)
    for part in range(2):
        put(vel[part], AT_VEL + 2 * part, 2)
    put(rate, AT_RATE, 2)

    @pl.when(lax.axis_index("comp") == 0)
    def _():
        msg0[AT_FLUX : AT_FLUX + ROWS] = flux[...]
        msg1[AT_FLUX : AT_FLUX + ROWS] = flux[...]

    @pl.when(lax.axis_index("comp") != 0)
    def _():
        for j in range(4):
            put(weight[j], AT_WEIGHT + 2 * j, 2)
            put(index[j].astype(jnp.float32), AT_INDEX + 2 * j, 2)

    put(west[0:ROWS], AT_WEST, 4)
    put(east[0:ROWS], AT_EAST, 4)
    for at in (AT_RATE + 2, AT_RATE + 4):
        msg0[at : at + 2] = jnp.zeros((2, COLS), jnp.float32)
        msg1[at : at + 2] = jnp.zeros((2, COLS), jnp.float32)


def row_messages(got0, got1):
    odd = lax.rem(lax.axis_index("lat"), 2)
    near = got0[1 - odd]
    far = got1[...]
    return jnp.where(odd == 1, near, far), jnp.where(odd == 1, far, near)


def transport_weights(east, north):
    def weights(v):
        near, far = v * (8.0 / 12.0), v * (1.0 / 12.0)
        return (-far, smoothing + near, smoothing - near, far)

    return weights(east), weights(north)


SHIFTS = (2, 1, -1, -2)


def along_longitude(own, side, weights):
    lane = lanes(own.shape[0])
    result = own * (1.0 - 4.0 * smoothing)
    for shift, factor in zip(SHIFTS, weights[0]):
        cut = lane >= COLS - shift if shift > 0 else lane < -shift
        result = result + factor * roll(jnp.where(cut, side, own), shift, 1)
    return result


def along_latitude(own, weights, rows):
    result = None
    for shift, factor in zip(SHIFTS, weights[1]):
        tap = factor * roll(own, shift, 0)[:rows]
        result = tap if result is None else result + tap
    return result


def factors(mix):
    inverses, ratios = [], []
    for level in range(LEV):
        pivot = 1.0
        if level < LEV - 1:
            pivot = pivot + mix[level]
        if level > 0:
            pivot = pivot + mix[level - 1] * (1.0 - ratios[-1])
        inverse = 1.0 / pivot
        inverses.append(inverse)
        if level < LEV - 1:
            ratios.append(mix[level] * inverse)
    return inverses, ratios


def solve(rhs, mix, inverses, ratios):
    values = []
    for level in range(LEV):
        source = rhs[level]
        if level > 0:
            source = mix[level - 1] * values[-1] if source is None else source + mix[level - 1] * values[-1]
        values.append(source * inverses[level])
    result = [None] * LEV
    result[-1] = values[-1]
    for level in range(LEV - 2, -1, -1):
        result[level] = values[level] + ratios[level] * result[level + 1]
    return result


def rim_of_levels(north, south, level):
    sub, block, odd = sublanes(), 8 * (level // 2), level % 2
    a, b = south[block : block + 8], north[block : block + 8]
    return jnp.where(sub < 4, roll(a, -4 * odd, 0), roll(b, 4 - 4 * odd, 0))


def side_of(west_tile, east_tile, at, width, rows):
    lane = lanes(rows)
    a, b = roll(east_tile[:rows], -at, 1), roll(west_tile[:rows], COLS - width - at, 1)
    return jnp.where(lane < width, a, jnp.where(lane >= COLS - width, b, 0.0))


IMPULSE = [1.0] + [None] * (LEV - 1)


def prepare_own(prev, mix, index, weight, inverse, unit, seen):
    own_mix = [mix[level] for level in range(LEV - 1)]
    inverses, ratios = factors(own_mix)
    impulse = solve(IMPULSE, own_mix, inverses, ratios)
    for level in range(LEV):
        inverse[level] = inverses[level]
        unit[level] = impulse[level]

    @pl.when(lax.axis_index("comp") == 0)
    def _():
        seen[...] = regrid_tile(prev[1], index, weight)


def own_early_kernel(*refs):
    @pl.when(starts_early())
    def _():
        prepare_own(*refs)


def own_late_kernel(prev, mix, index, weight, *both):
    @pl.when(jnp.logical_not(starts_early()))
    def _():
        prepare_own(prev, mix, index, weight, *both[len(both) // 2 :])


def prepare_side(
    state, vel, near, far, inverse, unit, side_mix, side_state, lon_own, lon_side
):
    west, east = sides(near[0:ROWS], far[0:ROWS])
    own_weights = transport_weights(vel[0], vel[1])
    side_weights = transport_weights(
        *(side_of(west, east, AT_VEL + 2 * part, 2, ROWS) for part in range(2))
    )
    for level in range(LEV):
        there = side_of(west, east, 4 * level, 4, ROWS)
        side_state[level] = there
        lon_own[level] = along_longitude(state[level], there, own_weights)
        lon_side[level] = along_longitude(there, state[level], side_weights)
    mixes = [side_of(west, east, AT_MIX + 2 * level, 2, ROWS) for level in range(LEV - 1)]
    inverses, ratios = factors(mixes)
    impulse = solve(IMPULSE, mixes, inverses, ratios)
    for level in range(LEV):
        inverse[level] = inverses[level]
        unit[level] = impulse[level]
        if level < LEV - 1:
            side_mix[level] = mixes[level]


def side_early_kernel(state, vel, near, far, *out):
    @pl.when(starts_early())
    def _():
        prepare_side(state, vel, near, far, *out)


def side_late_kernel(state, vel, near, far, *both):
    @pl.when(jnp.logical_not(starts_early()))
    def _():
        prepare_side(state, vel, near, far, *both[len(both) // 2 :])


def stored(inverse, mixes):
    inverses = [inverse[level] for level in range(LEV)]
    return inverses, [mixes[level] * inverses[level] for level in range(LEV - 1)]


def halo_step(state, mix, vel, columns, rows, inverse, side, before, before_side, unit_rim):
    west, east = column_messages(columns)
    north, south = row_messages(*rows)
    at_lat = lax.axis_index("lat")
    sub = sublanes()
    valid = ((sub < 4) & (at_lat < lax.axis_size("lat") - 1)) | ((sub >= 4) & (at_lat > 0))

    def rim2(at):
        block, offset = 8 * (at // 8), at % 8
        a, b = south[block : block + 8], north[block : block + 8]
        a, b = roll(a, -offset, 0), roll(b, 6 - offset, 0)
        return jnp.where(sub < 2, a, jnp.where(sub >= 6, b, 0.0))

    inverse_side, side_mix_ref, side_state, lon_own, lon_side = side
    a, b = south[AT_WEST : AT_WEST + 8], north[AT_WEST : AT_WEST + 8]
    west_rim = jnp.where(sub < 4, a, roll(b, 4, 0))
    east_rim = jnp.where(sub < 4, roll(a, 4, 0), b)
    own_mix = [mix[level] for level in range(LEV - 1)]
    side_mix = [side_mix_ref[level] for level in range(LEV - 1)]
    rim_mix = [rim2(AT_MIX + 2 * level) for level in range(LEV - 1)]
    rim_vel = [rim2(AT_VEL + 2 * part) for part in range(2)]
    own_weights = transport_weights(
        *(jnp.concatenate([vel[part], rim_vel[part]], axis=0) for part in range(2))
    )
    rim_weights = transport_weights(*rim_vel)
    side_weights = transport_weights(
        *(side_of(west, east, AT_VEL + 2 * part, 2, ROWS) for part in range(2))
    )
    rim_factors = factors(rim_mix)
    moved, moved_rim, moved_side = [], [], []
    for level in range(LEV):
        rim = rim_of_levels(north, south, level)
        side_rim = side_of(west_rim, east_rim, 4 * level, 4, 8)
        taps = along_latitude(jnp.concatenate([state[level], rim], axis=0), own_weights, 24)
        moved.append(lon_own[level] + taps[:ROWS])
        moved_rim.append(along_longitude(rim, side_rim, rim_weights) + taps[ROWS:])
        there = jnp.concatenate([side_state[level], side_rim], axis=0)
        moved_side.append(lon_side[level] + along_latitude(there, side_weights, ROWS))
    rim = solve(moved_rim, rim_mix, *rim_factors)
    impulse = solve(IMPULSE, rim_mix, *rim_factors)
    own = solve(moved, own_mix, *stored(inverse, own_mix))
    there = solve(moved_side, side_mix, *stored(inverse_side, side_mix))
    for level in range(LEV):
        before[level, 0:ROWS] = own[level]
        before[level, ROWS:] = jnp.where(valid, rim[level], 0.0)
        before_side[level] = there[level]
        unit_rim[level] = jnp.where(valid, impulse[level], 0.0)


def middle_kernel(
    state, mix, vel, rate, flux, early, late, to_early, to_late, row0, row1,
    inverse, unit, seen, inverse_side, side_mix, side_state, lon_own, lon_side,
    fluxes, before, before_side, unit_rim,
):
    columns, rows = (early, late, to_early, to_late), (row0, row1)
    side = (inverse_side, side_mix, side_state, lon_own, lon_side)

    halo_step(state, mix, vel, columns, rows, inverse, side, before, before_side, unit_rim)

    @pl.when(lax.axis_index("comp") == 0)
    def _():
        west, east = column_messages(columns)
        north, south = row_messages(*rows)
        top = before[0, 0:ROWS] + flux[...] * unit[0]
        fluxes[0:ROWS] = flux[...]
        fluxes[ROWS : 2 * ROWS] = west[ROWS:]
        fluxes[2 * ROWS : 3 * ROWS] = east[ROWS:]
        fluxes[3 * ROWS : 4 * ROWS] = north[AT_FLUX : AT_FLUX + ROWS]
        fluxes[4 * ROWS : 5 * ROWS] = south[AT_FLUX : AT_FLUX + ROWS]
        fluxes[5 * ROWS :] = rate[...] * (seen[...] - top)


def second_step_kernel(
    mix, vel, rate_in, index, weight, early, late, to_early, to_late, row0, row1,
    inverse, unit, unit_side, before, before_side, unit_rim, got, new_state, series,
):
    columns, rows = (early, late, to_early, to_late), (row0, row1)
    sub = sublanes()
    lane = lanes(ROWS)
    tables = [got[0, k * ROWS : (k + 1) * ROWS] for k in range(6)]
    own_mix = [mix[level] for level in range(LEV - 1)]

    def advance(force, force_rim, force_side, force1):
        weights = transport_weights(vel[0], vel[1])
        moved = []
        for level in range(LEV):
            tile = before[level, 0:ROWS] + force * unit[level]
            rim = before[level, ROWS:] + force_rim * unit_rim[level]
            there = before_side[level] + force_side * unit_side[level]
            if level == 0:
                top = tile
            own = jnp.concatenate([tile, rim], axis=0)
            taps = along_latitude(own, weights, ROWS)
            moved.append(along_longitude(tile, there, weights) + taps)
        moved[0] = moved[0] + force1
        solved = solve(moved, own_mix, *stored(inverse, own_mix))
        for level in range(LEV):
            new_state[level] = solved[level]
        return top, solved[0]

    @pl.when(lax.axis_index("comp") == 0)
    def _():
        rim = jnp.where(sub < 4, tables[4][0:8], tables[3][8:16])
        side = jnp.where(lane < 64, tables[2], tables[1])
        advance(tables[0], rim, side, tables[5])
        series[0] = tables[0]
        series[1] = tables[5]

    @pl.when(lax.axis_index("comp") != 0)
    def _():
        rate = rate_in[...]
        west, east = column_messages(columns)
        north, south = row_messages(*rows)

        def of_rows(message, table, place):
            index8 = message[AT_INDEX : AT_INDEX + 8].astype(jnp.int32)
            total = gather_cells(table, index8) * message[AT_WEIGHT : AT_WEIGHT + 8]
            total = total + roll(total, 4, 0)
            total = total + roll(total, 2, 0)
            block, offset = 8 * (AT_RATE // 8), AT_RATE % 8
            return roll(message[block : block + 8], place - offset, 0) * roll(total, place, 0)

        def of_columns(message, table, place):
            tile = message[0:ROWS]
            total = roll(gather_cells(table, tile.astype(jnp.int32)), AT_WEIGHT - AT_INDEX, 1) * tile
            total = total + roll(total, -4, 1)
            total = total + roll(total, -2, 1)
            return roll(tile, place - AT_RATE, 1) * roll(total, place - AT_WEIGHT, 1)

        rim = jnp.where(sub < 4, of_rows(south, tables[4], 0), of_rows(north, tables[3], 6))
        side = jnp.where(
            lane < 64, of_columns(east, tables[2], 0), of_columns(west, tables[1], COLS - 2)
        )
        force = rate * regrid_tile(tables[0], index, weight)
        force1 = rate * regrid_tile(tables[5], index, weight)
        top, last = advance(force, rim, side, force1)
        series[0] = top
        series[1] = last


def call(kernel, shapes, *args, scratch=(), place=pltpu.VMEM, aliases=None):
    return pl.pallas_call(
        kernel,
        out_shape=[s if hasattr(s, "dtype") else jax.ShapeDtypeStruct(s, jnp.float32) for s in shapes],
        in_specs=[pl.BlockSpec(memory_space=place)] * len(args),
        out_specs=[pl.BlockSpec(memory_space=pltpu.VMEM)] * len(shapes),
        scratch_shapes=list(scratch),
        compiler_params=pltpu.CompilerParams(vmem_limit_bytes=16 * 1024 * 1024),
        input_output_aliases=aliases or {},
        interpret=INTERPRET,
    )(*args)


def pairs(count, start, step):
    return [pair for i in range(start, count - 1, step) for pair in ((i, i + 1), (i + 1, i))]


def partners(count):
    return [[i, i + 1] for i in range(0, count, 2)]


def per_device(
    state, prev_surface, mixing, velocity, coupling, sea_mask, interp_index, interp_weight
):
    n_lat, n_lon = lax.axis_size("lat"), lax.axis_size("lon")
    given = (
        state[0], prev_surface, mixing[0], velocity[0],
        coupling[0], sea_mask[0], interp_index[0], interp_weight[0],
    )
    state, prev, mix, vel, couple, mask, index, weight = given
    tile = (ROWS, COLS)
    column_shape = (COL_MESSAGE, COLS)
    to_far, flux, rate, state, prev, mix, vel, index, weight = call(
        pack_columns_kernel,
        [column_shape, tile, tile, state, prev, mix, vel, index, weight],
        *(pltpu.with_memory_space_constraint(x, pltpu.HBM) for x in given), place=pltpu.HBM,
        scratch=[pltpu.VMEM(tile, couple.dtype), pltpu.VMEM(tile, mask.dtype), pltpu.SemaphoreType.DMA((8,))],
    )
    joints = range(1, n_lon, 2)
    sent = [((i, (i + 1) % n_lon) if i % 4 == 3 else (i + 1, i)) for i in joints]
    to_early = lax.ppermute(to_far, "lon", sent)
    fields = (state, mix, vel, rate, index, weight, flux)
    (to_near,) = call(near_early_kernel, [column_shape], *fields)
    early = lax.ppermute(to_near, "lon", pairs(n_lon, 0, 4))
    narrow = (LEV, ROWS, COLS)
    own_shapes = [narrow, narrow, tile]
    own = call(own_early_kernel, own_shapes, prev, mix, index, weight)
    to_late = lax.ppermute(to_far, "lon", [(j, i) for i, j in sent])
    (to_near,) = call(near_late_kernel, [column_shape], *fields)
    late = lax.ppermute(to_near, "lon", pairs(n_lon, 2, 4))
    columns = (early, late, to_early, to_late)
    row_shape = (ROW_MESSAGE, COLS)
    to_near, to_far = call(
        pack_rows_kernel, [row_shape, row_shape],
        state, mix, vel, rate, index, weight, flux, *columns,
    )
    row1 = lax.ppermute(to_far, "lat", pairs(n_lat, 1, 2))
    row0 = lax.all_gather(to_near, "lat", axis_index_groups=partners(n_lat))
    rows = (row0, row1)
    parts = [(LEV, 24, COLS), narrow, (LEV, 8, COLS)]
    inverse, unit, seen = call(
        own_late_kernel, own_shapes, prev, mix, index, weight, *own,
        aliases={4 + k: k for k in range(len(own_shapes))},
    )
    shapes = [narrow, narrow, (LEV - 1, ROWS, COLS), narrow, narrow, narrow]
    side = call(side_early_kernel, shapes, state, vel, early, to_early)
    inverse_side, unit_side, *side = call(
        side_late_kernel, shapes, state, vel, late, to_late, *side,
        aliases={4 + k: k for k in range(len(shapes))},
    )
    known = (inverse_side, *side)
    fluxes, *before = call(
        middle_kernel, [(6 * ROWS, COLS)] + parts,
        state, mix, vel, rate, flux, *columns, *rows, inverse, unit, seen, *known,
    )
    got = lax.all_gather(fluxes, "comp")
    new_state, series = call(
        second_step_kernel, [narrow, (NSTEP, ROWS, COLS)],
        mix, vel, rate, index, weight, *columns, *rows, inverse, unit, unit_side, *before, got,
    )
    return new_state[None], series[None]


def solution(mesh):
    in_specs = (
        P("comp", None, "lat", "lon"),
        P(None, "lat", "lon"),
        P("comp", None, "lat", "lon"),
        P("comp", None, "lat", "lon"),
        P("comp", "lat", "lon"),
        P("comp", "lat", "lon"),
        P("comp", None, "lat", "lon"),
        P("comp", None, "lat", "lon"),
    )
    out_specs = (P("comp", None, "lat", "lon"), P("comp", None, "lat", "lon"))

    return jax.shard_map(
        per_device, mesh=mesh, in_specs=in_specs, out_specs=out_specs, check_vma=False
    )
```

profile of v0, /device:TPU:88, one launch (start us, length us, event | category | flops | bytes accessed | tf_op | source)
XLA Modules:
  0.0 35.9 jit_solution(14826814309588661337)
XLA Ops:
  0.6 1.2 %shard_map.95 = (f32[32,128]{1,0:T(8,128)S(1)}, f32[16,128]{1,0:T(8,128)S(1)}, f32[16,128]{1,0:T(8,128)S(1)}, f32[12,16,128]{2,1,0:T(8,128)S(1)}, f32[2,16,128]{...) custom-call(f32[12,16,128]{2,1,0:T(8,128)} %bitcast.14, ...), custom_call_target="tpu_custom_call" | custom-call | tf_op jit(solution)/shard_map/pallas_call | solution.py:496
  1.9 0.2 shard_map.96
  2.0 6.1 %collective-permute-start = (f32[32,128]{1,0:T(8,128)S(1)}, f32[32,128]{1,0:T(8,128)S(1)}, u32[]{:S(2)}, u32[]{:S(2)}) collective-permute-start(f32[32,128]{1,0:T(8,128)S(1)} %shard_map.96), channel_id=1, source_target_pairs={{0,1},{1,0},{4,5},{5,4},{8,9},{9,8},{12,13},{13,12},{16,17},{17,16... | collective-permute-start | bytes 49160 | tf_op jit(solution)/shard_map/ppermute | solution.py:538
  8.1 1.3 %collective-permute-start.2 = (f32[32,128]{1,0:T(8,128)S(1)}, f32[32,128]{1,0:T(8,128)S(1)}, u32[]{:S(2)}, u32[]{:S(2)}) collective-permute-start(f32[32,128]{1,0:T(8,128)S(1)} %get-tuple-element.44), channel_id=1, source_target_pairs={{2,1},{3,4},{6,5},{7,8},{10,9},{11,12},{14,13},{15,0},{18,17},{19,... | collective-permute-start | bytes 49160 | tf_op jit(solution)/shard_map/ppermute | solution.py:535
  9.4 0.7 %collective-permute-start.1 = (f32[32,128]{1,0:T(8,128)S(1)}, f32[32,128]{1,0:T(8,128)S(1)}, u32[]{:S(2)}, u32[]{:S(2)}) collective-permute-start(f32[32,128]{1,0:T(8,128)S(1)} %shard_map.97), channel_id=1, source_target_pairs={{2,3},{3,2},{6,7},{7,6},{10,11},{11,10},{14,15},{15,14},{18,19},{1... | collective-permute-start | bytes 49160 | tf_op jit(solution)/shard_map/ppermute | solution.py:544
  10.1 10.2 %collective-permute-start.3 = (f32[32,128]{1,0:T(8,128)S(1)}, f32[32,128]{1,0:T(8,128)S(1)}, u32[]{:S(2)}, u32[]{:S(2)}) collective-permute-start(f32[32,128]{1,0:T(8,128)S(1)} %get-tuple-element.44), channel_id=1, source_target_pairs={{1,2},{4,3},{5,6},{8,7},{9,10},{12,11},{13,14},{0,15},{17,18},{20,... | collective-permute-start | bytes 49160 | tf_op jit(solution)/shard_map/ppermute | solution.py:542
  20.4 0.0 collective-permute-done.early.near
  20.4 0.0 collective-permute-done.2.to_early.far
  20.4 0.0 collective-permute-done.1.late.near
  20.4 1.4 %collective-permute-done.3.to_late.far = f32[32,128]{1,0:T(8,128)S(1)} collective-permute-done((f32[32,128]{1,0:T(8,128)S(1)}, f32[32,128]{1,0:T(8,128)S(1)}, u32[]{:S(2)}, u32[]{:S(2)}) %collective-permute-start.3) | collective-permute-done | bytes 16416 | tf_op jit(solution)/shard_map/ppermute | solution.py:542
  21.8 1.9 %collective-permute-start.4 = (f32[104,128]{1,0:T(8,128)S(1)}, f32[104,128]{1,0:T(8,128)S(1)}, u32[]{:S(2)}, u32[]{:S(2)}) collective-permute-start(f32[104,128]{1,0:T(8,128)S(1)} %get-tuple-element.46), channel_id=1, source_target_pairs={{16,32},{32,16},{48,64},{64,48},{80,96},{96,80},{112,128},{128,112... | collective-permute-start | bytes 159752 | tf_op jit(solution)/shard_map/ppermute | solution.py:551
  23.8 0.2 shard_map.99
  23.9 0.8 %shard_map.101 = (f32[12,16,128]{2,1,0:T(8,128)S(1)}, f32[12,16,128]{2,1,0:T(8,128)S(1)}, f32[11,16,128]{2,1,0:T(8,128)S(1)}, f32[12,16,128]{2,1,0:T(8,128)S(1)}...) custom-call(f32[12,16,128]{2,1,0:T(8,128)S(1)} %get-tuple-element.42.refs_0_.state, ...), custom_call_target="tpu_custom_call" | custom-call | tf_op jit(solution)/shard_map/pallas_call | solution.py:496
  24.8 4.4 %all-gather = f32[208,128]{1,0:T(8,128)S(1)} all-gather(f32[104,128]{1,0:T(8,128)S(1)} %get-tuple-element.45), channel_id=2, replica_groups={{0,16},{32,48},{64,80},{96,112},{128,144},{160,176},{192,208},{224,240}..., dimensions={0}, use_global_device_ids=true | all-gather | bytes 159744 | tf_op jit(solution)/shard_map/all_gather | solution.py:552
  29.2 0.0 collective-permute-done.4.row1
  29.2 0.3 shard_map.103
  29.6 4.8 %all-gather.1 = f32[192,128]{1,0:T(8,128)S(1)} all-gather(f32[96,128]{1,0:T(8,128)S(1)} %get-tuple-element.69), channel_id=3, replica_groups=mesh['comp'=2,'lat'=16,'lon'=16] {'comp'}, dimensions={0}, use_global_device_ids=true | all-gather | bytes 147456 | tf_op jit(solution)/shard_map/all_gather | solution.py:570
  34.3 1.6 %shard_map.104 = (f32[12,16,128]{2,1,0:T(8,128)}, f32[2,16,128]{2,1,0:T(8,128)}) custom-call(f32[11,16,128]{2,1,0:T(8,128)S(1)} %get-tuple-element.37.refs_1_.mix, f32[2,16,128]{2,1,0:T(8,128)S(1)} %get-tuple-element.38.refs_2_.vel, f32[16,128]{1,0:T(8,128)S(1)} %get-tuple-element.39.refs_3_.rate_in.rate, ...), custom_call_target="tpu_custom_call" | custom-call | tf_op jit(solution)/shard_map/pallas_call | solution.py:496
  (4 shorter events, 0.1 us)
Async XLA Ops:
  2.0 18.3 %collective-permute-start = (f32[32,128]{1,0:T(8,128)S(1)}, f32[32,128]{1,0:T(8,128)S(1)}, u32[]{:S(2)}, u32[]{:S(2)}) collective-permute-start(f32[32,128]{1,0:T(8,128)S(1)} %shard_map.96), channel_id=1, source_target_pairs={{0,1},{1,0},{4,5},{5,4},{8,9},{9,8},{12,13},{13,12},{16,17},{17,16... | collective-permute-start | bytes 49160 | tf_op jit(solution)/shard_map/ppermute | solution.py:538
  8.1 12.3 %collective-permute-start.2 = (f32[32,128]{1,0:T(8,128)S(1)}, f32[32,128]{1,0:T(8,128)S(1)}, u32[]{:S(2)}, u32[]{:S(2)}) collective-permute-start(f32[32,128]{1,0:T(8,128)S(1)} %get-tuple-element.44), channel_id=1, source_target_pairs={{2,1},{3,4},{6,5},{7,8},{10,9},{11,12},{14,13},{15,0},{18,17},{19,... | collective-permute-start | bytes 49160 | tf_op jit(solution)/shard_map/ppermute | solution.py:535
  9.4 10.9 %collective-permute-start.1 = (f32[32,128]{1,0:T(8,128)S(1)}, f32[32,128]{1,0:T(8,128)S(1)}, u32[]{:S(2)}, u32[]{:S(2)}) collective-permute-start(f32[32,128]{1,0:T(8,128)S(1)} %shard_map.97), channel_id=1, source_target_pairs={{2,3},{3,2},{6,7},{7,6},{10,11},{11,10},{14,15},{15,14},{18,19},{1... | collective-permute-start | bytes 49160 | tf_op jit(solution)/shard_map/ppermute | solution.py:544
  10.1 11.7 %collective-permute-start.3 = (f32[32,128]{1,0:T(8,128)S(1)}, f32[32,128]{1,0:T(8,128)S(1)}, u32[]{:S(2)}, u32[]{:S(2)}) collective-permute-start(f32[32,128]{1,0:T(8,128)S(1)} %get-tuple-element.44), channel_id=1, source_target_pairs={{1,2},{4,3},{5,6},{8,7},{9,10},{12,11},{13,14},{0,15},{17,18},{20,... | collective-permute-start | bytes 49160 | tf_op jit(solution)/shard_map/ppermute | solution.py:542
  21.8 7.4 %collective-permute-start.4 = (f32[104,128]{1,0:T(8,128)S(1)}, f32[104,128]{1,0:T(8,128)S(1)}, u32[]{:S(2)}, u32[]{:S(2)}) collective-permute-start(f32[104,128]{1,0:T(8,128)S(1)} %get-tuple-element.46), channel_id=1, source_target_pairs={{16,32},{32,16},{48,64},{64,48},{80,96},{96,80},{112,128},{128,112... | collective-permute-start | bytes 159752 | tf_op jit(solution)/shard_map/ppermute | solution.py:551
where the time goes:
time: 36.1 us; the launch traced here: 35.9 us
  starting transfers between devices  20.2 us (56%)
  blocking collectives  9.18 us (25%)
  Pallas kernels  4.34 us (12%)
  waiting for transfers between devices  1.4 us (4%)
  between operations  0.77 us (2%)
    ppermute x1, starting transfers between devices, per_device(): to_late = lax.ppermute(to_far, 'lon', [(j, i) for i, j in sent])  10.2 us
    ppermute x1, starting transfers between devices, per_device(): early = lax.ppermute(to_near, 'lon', pairs(n_lon, 0, 4))  6.09 us
    all_gather x1, blocking collectives, per_device(): got = lax.all_gather(fluxes, 'comp')  4.76 us
    all_gather x1, blocking collectives, per_device(): row0 = lax.all_gather(to_near, 'lat', axis_index_groups=partners(n_lat))  4.42 us
    pallas_call x10, Pallas kernels, call(): pl.pallas_call(kernel, out_shape=[s if hasattr(s, 'dtype') else jax.Shape...  4.34 us
    ppermute x1, starting transfers between devices, per_device(): row1 = lax.ppermute(to_far, 'lat', pairs(n_lat, 1, 2))  1.92 us
    ppermute x1, waiting for transfers between devices, per_device(): to_late = lax.ppermute(to_far, 'lon', [(j, i) for i, j in sent])  1.39 us
    ppermute x1, starting transfers between devices, per_device(): to_early = lax.ppermute(to_far, 'lon', sent)  1.29 us
  transfers between devices with their start and end apart: 5, of which 1 were waited for; matrix products, arithmetic and copies ran while one was open for 0% of the time, Pallas kernels for 3%

commit v1 on v0

--- a/solution.py
+++ b/solution.py
@@ -127,7 +127,7 @@
             )
         )
     ]
-    for move in moves:
+    for move in moves[3:] + moves[:3]:
         move.start()
     is_atmosphere = lax.axis_index("comp") == 0
     odd = lax.rem(lax.axis_index("lon"), 2) == 1
@@ -350,6 +350,24 @@
 def stored(inverse, mixes):
     inverses = [inverse[level] for level in range(LEV)]
     return inverses, [mixes[level] * inverses[level] for level in range(LEV - 1)]
+
+
+def top_step(state, mix, vel, rate, flux, columns, rows, inverse, unit, seen, lon_own, fluxes):
+    west, east = column_messages(columns)
+    north, south = row_messages(*rows)
+    weights = transport_weights(vel[0], vel[1])
+    moved = []
+    for level in range(LEV):
+        own = jnp.concatenate([state[level], rim_of_levels(north, south, level)], axis=0)
+        moved.append(lon_own[level] + along_latitude(own, weights, ROWS))
+    own_mix = [mix[level] for level in range(LEV - 1)]
+    top = solve(moved, own_mix, *stored(inverse, own_mix))[0] + flux[...] * unit[0]
+    fluxes[0:ROWS] = flux[...]
+    fluxes[ROWS : 2 * ROWS] = west[ROWS:]
+    fluxes[2 * ROWS : 3 * ROWS] = east[ROWS:]
+    fluxes[3 * ROWS : 4 * ROWS] = north[AT_FLUX : AT_FLUX + ROWS]
+    fluxes[4 * ROWS : 5 * ROWS] = south[AT_FLUX : AT_FLUX + ROWS]
+    fluxes[5 * ROWS :] = rate[...] * (seen[...] - top)
 
 
 def halo_step(state, mix, vel, columns, rows, inverse, side, before, before_side, unit_rim):
@@ -409,19 +427,11 @@
     columns, rows = (early, late, to_early, to_late), (row0, row1)
     side = (inverse_side, side_mix, side_state, lon_own, lon_side)
 
+    @pl.when(lax.axis_index("comp") == 0)
+    def _():
+        top_step(state, mix, vel, rate, flux, columns, rows, inverse, unit, seen, lon_own, fluxes)
+
     halo_step(state, mix, vel, columns, rows, inverse, side, before, before_side, unit_rim)
-
-    @pl.when(lax.axis_index("comp") == 0)
-    def _():
-        west, east = column_messages(columns)
-        north, south = row_messages(*rows)
-        top = before[0, 0:ROWS] + flux[...] * unit[0]
-        fluxes[0:ROWS] = flux[...]
-        fluxes[ROWS : 2 * ROWS] = west[ROWS:]
-        fluxes[2 * ROWS : 3 * ROWS] = east[ROWS:]
-        fluxes[3 * ROWS : 4 * ROWS] = north[AT_FLUX : AT_FLUX + ROWS]
-        fluxes[4 * ROWS : 5 * ROWS] = south[AT_FLUX : AT_FLUX + ROWS]
-        fluxes[5 * ROWS :] = rate[...] * (seen[...] - top)
 
 
 def second_step_kernel(

time: 36.1 us -> 36.1 us (level)
  no operation moved by 1% of the time
where the time goes in v1:
time: 36.1 us; the launch traced here: 35.8 us
  starting transfers between devices  20.2 us (56%)
  blocking collectives  9.18 us (25%)
  Pallas kernels  4.28 us (12%)
  waiting for transfers between devices  1.4 us (4%)
  between operations  0.76 us (2%)
    ppermute x1, starting transfers between devices, per_device(): to_late = lax.ppermute(to_far, 'lon', [(j, i) for i, j in sent])  10.2 us
    ppermute x1, starting transfers between devices, per_device(): early = lax.ppermute(to_near, 'lon', pairs(n_lon, 0, 4))  6.09 us
    all_gather x1, blocking collectives, per_device(): got = lax.all_gather(fluxes, 'comp')  4.76 us
    all_gather x1, blocking collectives, per_device(): row0 = lax.all_gather(to_near, 'lat', axis_index_groups=partners(n_lat))  4.42 us
    pallas_call x10, Pallas kernels, call(): pl.pallas_call(kernel, out_shape=[s if hasattr(s, 'dtype') else jax.Shape...  4.28 us
    ppermute x1, starting transfers between devices, per_device(): row1 = lax.ppermute(to_far, 'lat', pairs(n_lat, 1, 2))  1.92 us
    ppermute x1, waiting for transfers between devices, per_device(): to_late = lax.ppermute(to_far, 'lon', [(j, i) for i, j in sent])  1.39 us
    ppermute x1, starting transfers between devices, per_device(): to_early = lax.ppermute(to_far, 'lon', sent)  1.29 us
  transfers between devices with their start and end apart: 5, of which 1 were waited for; matrix products, arithmetic and copies ran while one was open for 0% of the time, Pallas kernels for 3%

profile of v1, /device:TPU:88, one launch (start us, length us, event | category | flops | bytes accessed | tf_op | source)
XLA Modules:
  0.0 35.8 jit_solution(941574957497514639)
XLA Ops:
  0.6 1.2 %shard_map.95 = (f32[32,128]{1,0:T(8,128)S(1)}, f32[16,128]{1,0:T(8,128)S(1)}, f32[16,128]{1,0:T(8,128)S(1)}, f32[12,16,128]{2,1,0:T(8,128)S(1)}, f32[2,16,128]{...) custom-call(f32[12,16,128]{2,1,0:T(8,128)} %bitcast.14, ...), custom_call_target="tpu_custom_call" | custom-call | tf_op jit(solution)/shard_map/pallas_call | solution.py:506
  1.8 0.2 shard_map.96
  2.0 6.1 %collective-permute-start = (f32[32,128]{1,0:T(8,128)S(1)}, f32[32,128]{1,0:T(8,128)S(1)}, u32[]{:S(2)}, u32[]{:S(2)}) collective-permute-start(f32[32,128]{1,0:T(8,128)S(1)} %shard_map.96), channel_id=1, source_target_pairs={{0,1},{1,0},{4,5},{5,4},{8,9},{9,8},{12,13},{13,12},{16,17},{17,16... | collective-permute-start | bytes 49160 | tf_op jit(solution)/shard_map/ppermute | solution.py:548
  8.1 1.3 %collective-permute-start.2 = (f32[32,128]{1,0:T(8,128)S(1)}, f32[32,128]{1,0:T(8,128)S(1)}, u32[]{:S(2)}, u32[]{:S(2)}) collective-permute-start(f32[32,128]{1,0:T(8,128)S(1)} %get-tuple-element.44), channel_id=1, source_target_pairs={{2,1},{3,4},{6,5},{7,8},{10,9},{11,12},{14,13},{15,0},{18,17},{19,... | collective-permute-start | bytes 49160 | tf_op jit(solution)/shard_map/ppermute | solution.py:545
  9.4 0.7 %collective-permute-start.1 = (f32[32,128]{1,0:T(8,128)S(1)}, f32[32,128]{1,0:T(8,128)S(1)}, u32[]{:S(2)}, u32[]{:S(2)}) collective-permute-start(f32[32,128]{1,0:T(8,128)S(1)} %shard_map.97), channel_id=1, source_target_pairs={{2,3},{3,2},{6,7},{7,6},{10,11},{11,10},{14,15},{15,14},{18,19},{1... | collective-permute-start | bytes 49160 | tf_op jit(solution)/shard_map/ppermute | solution.py:554
  10.1 10.2 %collective-permute-start.3 = (f32[32,128]{1,0:T(8,128)S(1)}, f32[32,128]{1,0:T(8,128)S(1)}, u32[]{:S(2)}, u32[]{:S(2)}) collective-permute-start(f32[32,128]{1,0:T(8,128)S(1)} %get-tuple-element.44), channel_id=1, source_target_pairs={{1,2},{4,3},{5,6},{8,7},{9,10},{12,11},{13,14},{0,15},{17,18},{20,... | collective-permute-start | bytes 49160 | tf_op jit(solution)/shard_map/ppermute | solution.py:552
  20.3 0.0 collective-permute-done.early.near
  20.3 0.0 collective-permute-done.2.to_early.far
  20.3 0.0 collective-permute-done.1.late.near
  20.3 1.4 %collective-permute-done.3.to_late.far = f32[32,128]{1,0:T(8,128)S(1)} collective-permute-done((f32[32,128]{1,0:T(8,128)S(1)}, f32[32,128]{1,0:T(8,128)S(1)}, u32[]{:S(2)}, u32[]{:S(2)}) %collective-permute-start.3) | collective-permute-done | bytes 16416 | tf_op jit(solution)/shard_map/ppermute | solution.py:552
  21.8 1.9 %collective-permute-start.4 = (f32[104,128]{1,0:T(8,128)S(1)}, f32[104,128]{1,0:T(8,128)S(1)}, u32[]{:S(2)}, u32[]{:S(2)}) collective-permute-start(f32[104,128]{1,0:T(8,128)S(1)} %get-tuple-element.46), channel_id=1, source_target_pairs={{16,32},{32,16},{48,64},{64,48},{80,96},{96,80},{112,128},{128,112... | collective-permute-start | bytes 159752 | tf_op jit(solution)/shard_map/ppermute | solution.py:561
  23.7 0.2 shard_map.99
  23.9 0.8 %shard_map.101 = (f32[12,16,128]{2,1,0:T(8,128)S(1)}, f32[12,16,128]{2,1,0:T(8,128)S(1)}, f32[11,16,128]{2,1,0:T(8,128)S(1)}, f32[12,16,128]{2,1,0:T(8,128)S(1)}...) custom-call(f32[12,16,128]{2,1,0:T(8,128)S(1)} %get-tuple-element.42.refs_0_.state, ...), custom_call_target="tpu_custom_call" | custom-call | tf_op jit(solution)/shard_map/pallas_call | solution.py:506
  24.7 4.4 %all-gather = f32[208,128]{1,0:T(8,128)S(1)} all-gather(f32[104,128]{1,0:T(8,128)S(1)} %get-tuple-element.45), channel_id=2, replica_groups={{0,16},{32,48},{64,80},{96,112},{128,144},{160,176},{192,208},{224,240}..., dimensions={0}, use_global_device_ids=true | all-gather | bytes 159744 | tf_op jit(solution)/shard_map/all_gather | solution.py:562
  29.2 0.0 collective-permute-done.4.row1
  29.2 0.3 shard_map.103
  29.5 4.8 %all-gather.1 = f32[192,128]{1,0:T(8,128)S(1)} all-gather(f32[96,128]{1,0:T(8,128)S(1)} %get-tuple-element.69), channel_id=3, replica_groups=mesh['comp'=2,'lat'=16,'lon'=16] {'comp'}, dimensions={0}, use_global_device_ids=true | all-gather | bytes 147456 | tf_op jit(solution)/shard_map/all_gather | solution.py:580
  34.3 1.6 %shard_map.104 = (f32[12,16,128]{2,1,0:T(8,128)}, f32[2,16,128]{2,1,0:T(8,128)}) custom-call(f32[11,16,128]{2,1,0:T(8,128)S(1)} %get-tuple-element.37.refs_1_.mix, f32[2,16,128]{2,1,0:T(8,128)S(1)} %get-tuple-element.38.refs_2_.vel, f32[16,128]{1,0:T(8,128)S(1)} %get-tuple-element.39.refs_3_.rate_in.rate, ...), custom_call_target="tpu_custom_call" | custom-call | tf_op jit(solution)/shard_map/pallas_call | solution.py:506
  (4 shorter events, 0.1 us)
Async XLA Ops:
  2.0 18.3 %collective-permute-start = (f32[32,128]{1,0:T(8,128)S(1)}, f32[32,128]{1,0:T(8,128)S(1)}, u32[]{:S(2)}, u32[]{:S(2)}) collective-permute-start(f32[32,128]{1,0:T(8,128)S(1)} %shard_map.96), channel_id=1, source_target_pairs={{0,1},{1,0},{4,5},{5,4},{8,9},{9,8},{12,13},{13,12},{16,17},{17,16... | collective-permute-start | bytes 49160 | tf_op jit(solution)/shard_map/ppermute | solution.py:548
  8.1 12.3 %collective-permute-start.2 = (f32[32,128]{1,0:T(8,128)S(1)}, f32[32,128]{1,0:T(8,128)S(1)}, u32[]{:S(2)}, u32[]{:S(2)}) collective-permute-start(f32[32,128]{1,0:T(8,128)S(1)} %get-tuple-element.44), channel_id=1, source_target_pairs={{2,1},{3,4},{6,5},{7,8},{10,9},{11,12},{14,13},{15,0},{18,17},{19,... | collective-permute-start | bytes 49160 | tf_op jit(solution)/shard_map/ppermute | solution.py:545
  9.4 10.9 %collective-permute-start.1 = (f32[32,128]{1,0:T(8,128)S(1)}, f32[32,128]{1,0:T(8,128)S(1)}, u32[]{:S(2)}, u32[]{:S(2)}) collective-permute-start(f32[32,128]{1,0:T(8,128)S(1)} %shard_map.97), channel_id=1, source_target_pairs={{2,3},{3,2},{6,7},{7,6},{10,11},{11,10},{14,15},{15,14},{18,19},{1... | collective-permute-start | bytes 49160 | tf_op jit(solution)/shard_map/ppermute | solution.py:554
  10.1 11.7 %collective-permute-start.3 = (f32[32,128]{1,0:T(8,128)S(1)}, f32[32,128]{1,0:T(8,128)S(1)}, u32[]{:S(2)}, u32[]{:S(2)}) collective-permute-start(f32[32,128]{1,0:T(8,128)S(1)} %get-tuple-element.44), channel_id=1, source_target_pairs={{1,2},{4,3},{5,6},{8,7},{9,10},{12,11},{13,14},{0,15},{17,18},{20,... | collective-permute-start | bytes 49160 | tf_op jit(solution)/shard_map/ppermute | solution.py:552
  21.8 7.4 %collective-permute-start.4 = (f32[104,128]{1,0:T(8,128)S(1)}, f32[104,128]{1,0:T(8,128)S(1)}, u32[]{:S(2)}, u32[]{:S(2)}) collective-permute-start(f32[104,128]{1,0:T(8,128)S(1)} %get-tuple-element.46), channel_id=1, source_target_pairs={{16,32},{32,16},{48,64},{64,48},{80,96},{96,80},{112,128},{128,112... | collective-permute-start | bytes 159752 | tf_op jit(solution)/shard_map/ppermute | solution.py:561
